TPU v7x, 32 devices: a whole 2x2x4 slice. The times are simulated.
32 devices in a mesh: grp: 2 (over x), px: 4 (over y, core), py: 4 (over z).
Axes of the slice: x: 2, y: 2, z: 4, core: 2. Of those that a mesh axis runs over, the one named last changes fastest.
Arguments:
- multiplier: float32 [3, 32, 16, 256, 256], P(None, 'py', None, ('grp', 'px')), may hold values from -6 to 6
- auxiliary: float32 [3, 32, 16, 256, 256], P(None, 'py', None, ('grp', 'px')), may hold values from -6 to 6
- density_start: float32 [16, 256, 256], P(None, ('grp', 'px')), may hold values from 0.5 to 2
- density_end: float32 [16, 256, 256], P(None, ('grp', 'px')), may hold values from 0.5 to 2
Outputs:
- multiplier_next: float32 [3, 32, 16, 256, 256], P(None, 'py', None, ('grp', 'px'))
- auxiliary_next: float32 [3, 32, 16, 256, 256], P(None, 'py', None, ('grp', 'px'))
All inputs are finite; a program needn't handle non-finite values.
Results may differ from a plain program's by a relative error of at most 0.0003.
Values sent between devices are 32-bit elements; how exact they have to be, the bound alone decides.
A program may use at most 128 MiB of HBM per device.

v0:
```python
import math
import jax
import jax.numpy as jnp
from jax import lax
from jax.sharding import PartitionSpec as P

NEWTON = 4
PENALTY = 1.0
PRECISE = lax.Precision.HIGHEST


def passed_along(value, axis, steps):
    count = lax.axis_size(axis)
    initial, last = (max(0, -steps), min(count, count - steps))
    return lax.ppermute(value, axis, [(source, source + steps) for source in range(initial, last)])


def from_behind(block, axis, distance):
    devices = range(lax.axis_size(axis))
    route = [((i - distance) % len(devices), i) for i in devices]
    return lax.ppermute(block, axis, route)


def cosine_table(levels):
    mode_index = lax.broadcasted_iota(jnp.int32, (levels, levels), 0)
    time_index = lax.broadcasted_iota(jnp.int32, (levels, levels), 1)
    phase_index = mode_index * (2 * time_index + 1) % (4 * levels)
    angles = phase_index.astype(jnp.float32) * (math.pi / (2 * levels))
    weights = jnp.where(mode_index == 0, math.sqrt(1.0 / levels), math.sqrt(2.0 / levels))
    return weights * jnp.cos(angles)


def difference_table(cosine):
    levels = cosine.shape[0]
    later = jnp.concatenate([cosine[:, 1:], jnp.zeros_like(cosine[:, :1])], axis=1)
    time_index = lax.broadcasted_iota(jnp.int32, (levels, levels), 1)
    return jnp.where(time_index < levels - 1, later - cosine, 0.0)


def hartley_table(length):
    row_index = lax.broadcasted_iota(jnp.int32, (length, length), 0)
    col_index = lax.broadcasted_iota(jnp.int32, (length, length), 1)
    phase_index = row_index * col_index % length
    angles = phase_index.astype(jnp.float32) * (2.0 * math.pi / length)
    return (jnp.cos(angles) + jnp.sin(angles)) / math.sqrt(length)


def spatial(field, hartley_rows, hartley_cols):
    field = jnp.einsum("ctbxy,kx->ctbky", field, hartley_rows, precision=PRECISE)
    return jnp.einsum("ctbxy,ky->ctbxk", field, hartley_cols, precision=PRECISE)


def eigenvalues(levels, row_start, row_total, row_count, col_count):
    time_modes = lax.broadcasted_iota(jnp.int32, (levels, 1, 1, 1), 0).astype(jnp.float32)
    row_modes = (row_start + lax.broadcasted_iota(jnp.int32, (1, 1, row_total, 1), 2)).astype(
        jnp.float32
    )
    col_modes = lax.broadcasted_iota(jnp.int32, (1, 1, 1, col_count), 3).astype(jnp.float32)
    time_part = 4.0 * jnp.sin(time_modes * (math.pi / (2 * levels))) ** 2
    row_part = 4.0 * jnp.sin(row_modes * (math.pi / row_count)) ** 2
    col_part = 4.0 * jnp.sin(col_modes * (math.pi / col_count)) ** 2
    return time_part + row_part + col_part


def project(target):
    time_part = target[0]
    space_first = target[1]
    space_second = target[2]
    kinetic = 0.5 * (space_first * space_first + space_second * space_second)
    offset_one = 1.0 + time_part
    scaling = jnp.maximum(offset_one, 1.0) + jnp.cbrt(kinetic)
    for newton_step in range(NEWTON):
        residue = scaling * scaling * (scaling - offset_one) - kinetic
        derivative = scaling * (3.0 * scaling - 2.0 * offset_one)
        scaling = jnp.maximum(scaling - residue / derivative, 1.0)
    feasible = time_part + kinetic <= 0.0
    return jnp.stack(
        [
            jnp.where(feasible, time_part, time_part - (scaling - 1.0)),
            jnp.where(feasible, space_first, space_first / scaling),
            jnp.where(feasible, space_second, space_second / scaling),
        ]
    )


def local(multiplier, auxiliary, density_start, density_end):
    levels_here = multiplier.shape[1]
    levels = levels_here * lax.axis_size("py")
    first_level = lax.axis_index("py") * levels_here
    level_index = first_level + lax.broadcasted_iota(jnp.int32, (levels_here, 1, 1, 1), 0)
    offset_field = auxiliary - multiplier / PENALTY
    offset_time = jnp.where(level_index == levels - 1, 0.0, offset_field[0])
    boundary = jnp.where(level_index == 0, -density_start / PENALTY, 0.0) + jnp.where(
        level_index == levels - 1, density_end / PENALTY, 0.0
    )
    offset_second = offset_field[2]
    source = jnp.roll(offset_second, 1, axis=3) - offset_second + boundary
    before = passed_along(offset_time[levels_here - 1 :], "py", 1)
    earlier = jnp.concatenate([before, offset_time[: levels_here - 1]], axis=0)
    offset_along = offset_field[1]
    rows_here = offset_along.shape[2]
    left_rim = from_behind(offset_along[:, :, rows_here - 1 :, :], ("grp", "px"), 1)
    beside = jnp.concatenate([left_rim, offset_along[:, :, : rows_here - 1, :]], axis=2)
    payload = (earlier - offset_time + beside - offset_along + source)[None]
    pencil = lax.all_to_all(payload, ("grp", "px"), split_axis=2, concat_axis=3, tiled=True)
    row_count = pencil.shape[3]
    col_count = pencil.shape[4]
    hartley_rows = hartley_table(row_count)
    hartley_cols = hartley_table(col_count)
    spectral = spatial(pencil, hartley_rows, hartley_cols)
    mode_data = lax.all_to_all(spectral, "py", split_axis=3, concat_axis=1, tiled=True)
    cosine = cosine_table(levels)
    difference = difference_table(cosine)
    rhs_modes = jnp.einsum("kt,tbxy->kbxy", cosine, mode_data[0], precision=PRECISE)
    rows_mode = mode_data.shape[3]
    eigen = eigenvalues(levels, lax.axis_index("py") * rows_mode, rows_mode, row_count, col_count)
    positive = eigen > 0.0
    inverse = jnp.where(positive, 1.0 / jnp.where(positive, eigen, 1.0), 0.0)
    potential_modes = rhs_modes * inverse
    potential = jnp.einsum("kt,kbxy->tbxy", cosine, potential_modes, precision=PRECISE)
    time_rate = jnp.einsum("kt,kbxy->tbxy", difference, potential_modes, precision=PRECISE)
    returned = lax.all_to_all(
        jnp.stack([potential, time_rate]), "py", split_axis=1, concat_axis=3, tiled=True
    )
    space_values = spatial(returned, hartley_rows, hartley_cols)
    plane_potential = space_values[0]
    gradient = jnp.stack(
        [
            space_values[1],
            jnp.roll(plane_potential, -1, axis=2) - plane_potential,
            jnp.roll(plane_potential, -1, axis=3) - plane_potential,
        ]
    )
    slab_gradient = lax.all_to_all(gradient, ("grp", "px"), split_axis=3, concat_axis=2, tiled=True)
    target = slab_gradient + multiplier / PENALTY
    auxiliary_next = project(target)
    multiplier_next = multiplier + PENALTY * (slab_gradient - auxiliary_next)
    return (multiplier_next, auxiliary_next)


def solution(mesh):
    placed = (
        P(None, "py", None, ("grp", "px"), None),
        P(None, "py", None, ("grp", "px"), None),
        P(None, ("grp", "px"), None),
        P(None, ("grp", "px"), None),
    )
    return jax.shard_map(
        local,
        mesh=mesh,
        in_specs=placed,
        out_specs=(
            P(None, "py", None, ("grp", "px"), None),
            P(None, "py", None, ("grp", "px"), None),
        ),
        check_vma=False,
    )
```

profile of v0, /device:TPU:0, one launch (start us, length us, event | category | flops | bytes accessed | tf_op | source)
XLA Modules:
  0.0 775.5 jit_solution(9766000139064356499)
XLA Ops:
  0.6 22.9 %copy_subtract_fusion = f32[3,8,16,32,256]{4,2,1,3,0:T(8,128)S(1)} fusion(f32[3,8,16,32,256]{4,3,2,1,0:T(8,128)} %param.5, f32[3,8,16,32,256]{4,3,2,1,0:T(8,128)} %param.4), kind=kLoop, calls=%fused_computation.3 | loop fusion | flops 3145728 | bytes 37748736 | tf_op jit(solution)/shard_map/sub | solution.py:91
  25.7 5.8 collective-permute-start
  49.0 10.4 %fusion.4 = f32[1,8,16,32,256]{4,2,1,3,0:T(8,128)S(1)} fusion(f32[1,7,16,32,256]{4,2,1,3,0:T(8,128)} %slice_bitcast_fusion.7, f32[1,1,16,32,256]{4,2,1,3,0:T(8,128)} %bitcast.9, f32[1,8,16,31,256]{4,2,1,3,0:T(8,128)} %slice_bitcast_fusion.3, f32[1,8,16,1,256]{4,2,1,3,0:T(8,128)S(1)} %bitcast.104, f32[1,8,16,32,255]{4,2,1,3,0:T(8,128)} %slice_bitcast_fusion.2, ...), kind=kLoop, calls=%fused_computation.18 | loop fusion | flops 13631488 | bytes 30408720 | tf_op jit(solution)/shard_map/add | solution.py:104
  61.8 52.6 %all_to_all.66 = f32[1,8,16,32,256]{4,1,3,0,2:T(8,128)S(1)} all-to-all(f32[1,8,16,32,256]{4,1,3,0,2:T(8,128)S(1)} %copy.75), channel_id=1, replica_groups=mesh['grp'=2,'px'=4,'py'=4] {'grp','px'}, dimensions={2} | all-to-all | bytes 8388608 | tf_op jit(solution)/shard_map/all_to_all | solution.py:105
  125.2 5.4 copy.77
  130.6 4.9 all-to-all-start.1
  136.3 92.5 %all-to-all-done.1 = f32[1,8,2,256,256]{4,2,1,0,3:T(2,128)} async-done(((f32[1,8,2,256,256]{4,2,1,0,3:T(2,128)}), f32[1,8,2,256,256]{4,2,1,0,3:T(2,128)}, u32[]{:S(2)}, u32[]{:S(2)}) %all-to-all-start.1) | async-done | bytes 4194336 | tf_op jit(solution)/shard_map/all_to_all | solution.py:111
  228.8 6.0 fusion.6
  244.7 5.3 copy.80
  249.9 185.3 %all_to_all.67 = f32[2,32,2,64,256]{4,3,2,0,1:T(8,128)S(1)} all-to-all(f32[2,32,2,64,256]{4,3,2,0,1:T(8,128)S(1)} %copy.80), channel_id=1, replica_groups=mesh['grp'=2,'px'=4,'py'=4] {'py'}, dimensions={1} | all-to-all | bytes 16777216 | tf_op jit(solution)/shard_map/all_to_all | solution.py:122
  436.4 9.7 %fusion.45 = f32[256,2,8,2,256]{4,0,3,2,1:T(8,128)S(1)} fusion(f32[2,8,2,256,256]{4,3,2,1,0:T(8,128)S(1)} %bitcast.100), kind=kOutput, calls=%fused_computation.74 | convolution fusion | flops 6443499520 | bytes 16777216 | tf_op jit(solution)/shard_map/ctbxy,kx->ctbky/dot_general | solution.py:49
  446.1 8.2 %fusion = f32[2,8,2,256,256]{4,3,2,1,0:T(8,128)S(1)} fusion(f32[256,2,8,2,256]{4,0,3,2,1:T(8,128)S(1)} %fusion.45), kind=kOutput, calls=%fused_computation.7 | convolution fusion | flops 6443499520 | bytes 16777216 | tf_op jit(solution)/shard_map/ctbxy,ky->ctbxk/dot_general | solution.py:50
  464.7 9.9 %fusion.104 = (f32[1,8,2,256,256]{4,3,2,1,0:T(8,128)S(1)}, f32[1,8,2,256,256]{4,3,2,1,0:T(8,128)}, f32[1,8,2,256,256]{4,3,2,1,0:T(8,128)}) fusion(f32[2,8,2,256,256]{4,3,2,1,0:T(8,128)} %copy-done.1, f32[1,8,2,1,256]{4,3,2,1,0:T(1,128)S(1)} %slice_bitcast_fusion.8, f32[1,8,2,255,256]{4,3,2,1,0:T(8,128)} %slice_bitcast_fusion.1, ...), kind=kLoop, calls=%fused_computation.143 | loop fusion | flops 4194304 | bytes 29360128 | tf_op jit(solution)/shard_map/slice | solution.py:129
  474.6 9.7 %pad_maximum_fusion = f32[3,8,2,256,256]{4,3,2,1,0:T(8,128)} fusion(f32[1,8,2,256,256]{4,3,2,1,0:T(8,128)} %get-tuple-element.21, f32[1,8,2,256,256]{4,3,2,1,0:T(8,128)} %get-tuple-element.20, f32[1,8,2,256,256]{4,3,2,1,0:T(8,128)S(1)} %get-tuple-element.19), kind=kLoop, calls=%fused_computation | loop fusion | flops 6291456 | bytes 25165824 | tf_op jit(solution)/shard_map/stack | solution.py:127
  484.3 21.0 %copy.85 = f32[3,8,2,256,256]{4,2,1,0,3:T(2,128)S(1)} copy(f32[3,8,2,256,256]{4,3,2,1,0:T(8,128)} %pad_maximum_fusion) | data formatting | bytes 25165824 | tf_op jit(solution)/shard_map/stack | solution.py:127
  505.3 143.1 %all_to_all.68 = f32[3,8,2,256,256]{4,2,1,0,3:T(2,128)S(1)} all-to-all(f32[3,8,2,256,256]{4,2,1,0,3:T(2,128)S(1)} %copy.85), channel_id=1, replica_groups=mesh['grp'=2,'px'=4,'py'=4] {'grp','px'}, dimensions={3} | all-to-all | bytes 25165824 | tf_op jit(solution)/shard_map/all_to_all | solution.py:134
  648.4 8.0 %copy.107 = f32[3,8,2,8,32,256]{5,2,3,1,4,0:T(2,128)} copy(f32[3,8,2,8,32,256]{5,2,1,0,4,3:T(2,128)S(1)} %bitcast.97) | data formatting | bytes 25165824 | tf_op jit(solution)/shard_map/all_to_all | solution.py:134
  656.4 15.7 %all_to_all.61 = f32[3,8,16,32,256]{4,2,1,3,0:T(8,128)} reshape(f32[3,8,8,2,32,256]{5,3,2,1,4,0:T(2,128)} %bitcast.98) | data formatting | bytes 25165824 | tf_op jit(solution)/shard_map/all_to_all | solution.py:134
  672.1 18.4 %copy_add_fusion = f32[3,8,16,32,256]{4,2,1,3,0:T(8,128)} fusion(f32[3,8,16,32,256]{4,2,1,3,0:T(8,128)} %all_to_all.61, f32[3,8,16,32,256]{4,3,2,1,0:T(8,128)} %param.4), kind=kLoop, calls=%fused_computation.5 | loop fusion | flops 3145728 | bytes 37748736 | tf_op jit(solution)/shard_map/add | solution.py:135
  690.5 14.7 %subtract_select_fusion = (f32[1,8,16,32,256]{4,2,1,3,0:T(8,128)}, f32[1,8,16,32,256]{4,2,1,3,0:T(8,128)S(1)}, pred[1,8,16,32,256]{4,2,1,3,0:T(8,128)(4,1)S(1)}) fusion(f32[3,8,16,32,256]{4,2,1,3,0:T(8,128)} %copy_add_fusion), kind=kLoop, calls=%fused_computation.11 | loop fusion | flops 55574528 | bytes 22020096 | tf_op jit(solution)/shard_map/jit(_where)/select_n | solution.py:79
  705.3 7.5 divide_select_fusion.1
  714.1 20.6 %pad_maximum_fusion.1 = (f32[3,8,16,32,256]{4,2,1,3,0:T(8,128)}, f32[3,8,16,32,256]{4,2,1,3,0:T(8,128)}) fusion(f32[1,8,16,32,256]{4,2,1,3,0:T(8,128)} %get-tuple-element.14, f32[1,8,16,32,256]{4,2,1,3,0:T(8,128)} %get-tuple-element.13, f32[1,8,16,32,256]{4,2,1,3,0:T(8,128)} %get-tuple-element.10, f32[3,8,16,32,256]{4,2,1,3,0:T(8,128)S(1)} %bitcast.96, ...), kind=kLoop, calls=%fused_computation.1 | loop fusion | flops 12582912 | bytes 62914560 | tf_op jit(solution)/shard_map/stack | solution.py:77
  734.8 20.2 %copy.90 = f32[3,8,16,32,256]{4,3,2,1,0:T(8,128)} copy(f32[3,8,16,32,256]{4,2,1,3,0:T(8,128)} %get-tuple-element.15) | data formatting | bytes 25165824
  754.9 20.4 %copy.89 = f32[3,8,16,32,256]{4,3,2,1,0:T(8,128)} copy(f32[3,8,16,32,256]{4,2,1,3,0:T(8,128)} %get-tuple-element.16) | data formatting | bytes 25165824
  (67 shorter events, 56.1 us)
Async XLA Ops:
  23.6 11.3 %copy-start = (f32[3,8,16,32,256]{4,2,1,3,0:T(8,128)}, f32[3,8,16,32,256]{4,2,1,3,0:T(8,128)S(1)}, u32[]{:S(2)}) copy-start(f32[3,8,16,32,256]{4,2,1,3,0:T(8,128)S(1)} %copy_subtract_fusion) | copy-start | bytes 37748740
  25.7 23.2 %collective-permute-start = (f32[1,16,32,256]{3,1,0,2:T(8,128)}, f32[1,16,32,256]{3,1,0,2:T(8,128)}, u32[]{:S(2)}, u32[]{:S(2)}) collective-permute-start(f32[1,16,32,256]{3,1,0,2:T(8,128)} %slice.83), channel_id=1, source_target_pairs={{0,1},{1,2},{2,3},{4,5},{5,6},{6,7},{8,9},{9,10},{10,11},{12,13},{... | collective-permute-start | bytes 1572872 | tf_op jit(solution)/shard_map/ppermute | solution.py:15
  35.8 13.1 %collective-permute-start.1 = (f32[8,16,1,256]{3,1,0,2:T(8,128)S(1)}, f32[8,16,1,256]{3,1,0,2:T(8,128)S(1)}, u32[]{:S(2)}, u32[]{:S(2)}) collective-permute-start(f32[8,16,1,256]{3,1,0,2:T(8,128)S(1)} %slice.86), channel_id=1, source_target_pairs={{28,0},{0,4},{4,8},{8,12},{12,16},{16,20},{20,24},{24,28},{29,1},{... | collective-permute-start | bytes 393224 | tf_op jit(solution)/shard_map/ppermute | solution.py:21
  36.1 3.7 copy-start.2
  42.3 2.8 copy-start.3
  44.5 1.0 copy-start.4
  130.6 98.2 %all-to-all-start.1 = ((f32[1,8,2,256,256]{4,2,1,0,3:T(2,128)}), f32[1,8,2,256,256]{4,2,1,0,3:T(2,128)}, u32[]{:S(2)}, u32[]{:S(2)}) async-start(f32[1,8,2,256,256]{4,2,1,0,3:T(2,128)} %copy.77), calls=%async_computation.1 | async-start | bytes 8388608 | tf_op jit(solution)/shard_map/all_to_all | solution.py:111
  454.2 3.4 copy-start.1
  690.5 22.3 %slice-start = ((s8[12582912]{0:T(1024)(128)(4,1)}), s8[4194304]{0:T(1024)(128)(4,1)S(1)}, s32[]{:S(2)}) async-start(s8[12582912]{0:T(1024)(128)(4,1)} %bitcast.93), calls=%async_computation.4 | async-start | bytes 8388608
  690.5 22.3 %slice-start.1 = ((s8[12582912]{0:T(1024)(128)(4,1)}), s8[4194304]{0:T(1024)(128)(4,1)S(1)}, s32[]{:S(2)}) async-start(s8[12582912]{0:T(1024)(128)(4,1)} %bitcast.93), calls=%async_computation.5 | async-start | bytes 8388608
  690.5 22.3 %slice-start.3 = ((s8[12582912]{0:T(1024)(128)(4,1)}), s8[4194304]{0:T(1024)(128)(4,1)S(1)}, s32[]{:S(2)}) async-start(s8[12582912]{0:T(1024)(128)(4,1)} %bitcast.95), calls=%async_computation.7 | async-start | bytes 8388608
  690.5 22.3 %slice-start.4 = ((s8[12582912]{0:T(1024)(128)(4,1)}), s8[4194304]{0:T(1024)(128)(4,1)S(1)}, s32[]{:S(2)}) async-start(s8[12582912]{0:T(1024)(128)(4,1)} %bitcast.95), calls=%async_computation.8 | async-start | bytes 8388608
  705.3 7.5 slice-start.2
  705.3 8.8 %slice-start.5 = ((s8[12582912]{0:T(1024)(128)(4,1)}), s8[4194304]{0:T(1024)(128)(4,1)S(1)}, s32[]{:S(2)}) async-start(s8[12582912]{0:T(1024)(128)(4,1)} %bitcast.95), calls=%async_computation.9 | async-start | bytes 8388608
where the time goes:
time: 783 us; the launch traced here: 776 us
  blocking collectives  381 us (49%)
  local copies, waits for them, and re-layouts  131 us (17%)
  other arithmetic  118 us (15%)
  waiting for transfers between devices  92.5 us (12%)
  matrix products  41.5 us (5%)
  starting transfers between devices  10.9 us (1%)
    all_to_all x1, blocking collectives, local(): lax.all_to_all(jnp.stack([potential, time_rate]), 'py', split_axis=1, con...  185 us
    all_to_all x1, blocking collectives, local(): lax.all_to_all(gradient, ('grp', 'px'), split_axis=3, concat_axis=2, tile...  143 us
    all_to_all x1, waiting for transfers between devices, local(): lax.all_to_all(spectral, 'py', split_axis=3, concat_axis=1, tiled=True)  92.5 us
    all_to_all x1, blocking collectives, local(): lax.all_to_all(payload, ('grp', 'px'), split_axis=2, concat_axis=3, tiled...  52.6 us
    unnamed x25, local copies, waits for them, and re-layouts  46.4 us
    all_to_all x2, local copies, waits for them, and re-layouts, local(): lax.all_to_all(gradient, ('grp', 'px'), split_axis=3, concat_axis=2, tile...  23.7 us
    sub x1, other arithmetic, local(): offset_field = auxiliary - multiplier / PENALTY  22.9 us
    another operation x1, local copies, waits for them, and re-layouts, local(): jnp.stack([space_values[1], jnp.roll(plane_potential, -1, axis=2) - plane...  21 us
  transfers between devices with their start and end apart: 3, of which 1 were waited for; matrix products, arithmetic and copies ran while one was open for 2% of the time, Pallas kernels for 0%

commit v1 on v0

--- a/solution.py
+++ b/solution.py
@@ -7,6 +7,18 @@
 NEWTON = 4
 PENALTY = 1.0
 PRECISE = lax.Precision.HIGHEST
+
+
+def cut_along(shard, dim, size):
+    shape = shard.shape
+    parts = shard.reshape(*shape[:dim], size, shape[dim] // size, *shape[dim + 1 :])
+    return jnp.moveaxis(parts, dim, 0)
+
+
+def laid_out(tiles, dim):
+    dims = list(tiles.shape[1:])
+    dims[dim] *= tiles.shape[0]
+    return jnp.moveaxis(tiles, 0, dim).reshape(dims)
 
 
 def passed_along(value, axis, steps):
@@ -102,7 +114,16 @@
     left_rim = from_behind(offset_along[:, :, rows_here - 1 :, :], ("grp", "px"), 1)
     beside = jnp.concatenate([left_rim, offset_along[:, :, : rows_here - 1, :]], axis=2)
     payload = (earlier - offset_time + beside - offset_along + source)[None]
-    pencil = lax.all_to_all(payload, ("grp", "px"), split_axis=2, concat_axis=3, tiled=True)
+    size, place = (lax.axis_size(("grp", "px")), lax.axis_index(("grp", "px")))
+    pieces = cut_along(payload, 2, size)
+    gathered = [pieces[place]]
+    for step in range(1, size):
+        sent = pieces[place ^ step]
+        gathered.append(
+            lax.ppermute(sent, ("grp", "px"), [(i_2, i_2 ^ step) for i_2 in range(size)])
+        )
+    pieces = jnp.stack(gathered)[place ^ jnp.arange(size)]
+    pencil = laid_out(pieces, 3)
     row_count = pencil.shape[3]
     col_count = pencil.shape[4]
     hartley_rows = hartley_table(row_count)

time: 783 us -> 761 us (0.972)
  blocking collectives: 381 us -> 330 us
  waiting for transfers between devices: 92.5 us -> 131 us
  local copies, waits for them, and re-layouts: 131 us -> 116 us
  starting transfers between devices: 10.9 us -> 18.9 us
    all_to_all x1 -> x0, blocking collectives: 52.6 us -> none  [local(): lax.all_to_all(payload, ('grp', 'px'), split_axis=2, concat_axis=3, tiled...]
    ppermute x0 -> x7, waiting for transfers between devices: none -> 38 us  [local(): lax.ppermute(sent, ('grp', 'px'), [(i_2, i_2 ^ step) for i_2 in range(siz...]
    unnamed x25 -> x35, local copies, waits for them, and re-layouts: 46.4 us -> 20 us
    another operation x1 -> x0, other arithmetic: 20.6 us -> none  [project(): jnp.stack([jnp.where(feasible, time_part, time_part - (scaling - 1.0)), j...]
    add x0 -> x1, other arithmetic: none -> 14.4 us  [local(): multiplier_next = multiplier + PENALTY * (slab_gradient - auxiliary_next)]
    slice x0 -> x2, local copies, waits for them, and re-layouts: none -> 9.03 us  [the longest x1 6.39 us: local(): offset_time = jnp.where(level_index == levels - 1, 0.0, offset_field[0])]
    add x1, other arithmetic: 10.4 us -> 18.9 us  [local(): payload = (earlier - offset_time + beside - offset_along + source)[None]]
    all_to_all x2 -> x1, local copies, waits for them, and re-layouts: 23.7 us -> 16.6 us  [local(): lax.all_to_all(gradient, ('grp', 'px'), split_axis=3, concat_axis=2, tile...]
  transfers between devices with their start and end apart: 3 -> 10, of which waited for: 1 -> 4; matrix products, arithmetic and copies ran while one was open for 2% -> 5% of each run, Pallas kernels for 0% -> 0%
where the time goes in v1:
time: 761 us; the launch traced here: 754 us
  blocking collectives  330 us (43%)
  waiting for transfers between devices  131 us (17%)
  other arithmetic  116 us (15%)
  local copies, waits for them, and re-layouts  116 us (15%)
  matrix products  41.5 us (5%)
  starting transfers between devices  18.9 us (2%)
    all_to_all x1, blocking collectives, local(): lax.all_to_all(jnp.stack([potential, time_rate]), 'py', split_axis=1, con...  186 us
    all_to_all x1, blocking collectives, local(): lax.all_to_all(gradient, ('grp', 'px'), split_axis=3, concat_axis=2, tile...  144 us
    all_to_all x1, waiting for transfers between devices, local(): lax.all_to_all(spectral, 'py', split_axis=3, concat_axis=1, tiled=True)  93.2 us
    ppermute x7, waiting for transfers between devices, local(): lax.ppermute(sent, ('grp', 'px'), [(i_2, i_2 ^ step) for i_2 in range(siz...  38 us
    sub x1, other arithmetic, local(): offset_field = auxiliary - multiplier / PENALTY  22.9 us
    another operation x1, local copies, waits for them, and re-layouts, local(): jnp.stack([space_values[1], jnp.roll(plane_potential, -1, axis=2) - plane...  21 us
    unnamed x35, local copies, waits for them, and re-layouts  20 us
    add x1, other arithmetic, local(): payload = (earlier - offset_time + beside - offset_along + source)[None]  18.9 us
  transfers between devices with their start and end apart: 10, of which 4 were waited for; matrix products, arithmetic and copies ran while one was open for 5% of the time, Pallas kernels for 0%

profile of v1, /device:TPU:0, one launch (start us, length us, event | category | flops | bytes accessed | tf_op | source)
XLA Modules:
  0.0 754.2 jit_solution(4864248409760097866)
XLA Ops:
  0.6 22.9 %copy_subtract_fusion = f32[3,8,16,32,256]{4,1,2,3,0:T(8,128)S(1)} fusion(f32[3,8,16,32,256]{4,3,2,1,0:T(8,128)} %param.4, f32[3,8,16,32,256]{4,3,2,1,0:T(8,128)} %param.5), kind=kLoop, calls=%fused_computation.3 | loop fusion | flops 3145728 | bytes 37748736 | tf_op jit(solution)/shard_map/sub | solution.py:103
  27.5 5.8 collective-permute-start
  33.3 6.4 fusion.105
  56.4 6.5 copy.78
  64.5 18.9 %fusion.4 = f32[1,8,8,2,32,256]{5,4,3,1,2,0:T(8,128)S(1)} fusion(f32[1,7,8,2,32,256]{5,4,3,1,2,0:T(8,128)} %copy.71, f32[1,1,8,2,32,256]{5,4,3,1,2,0:T(8,128)S(1)} %bitcast.144, f32[1,8,8,2,31,256]{5,4,3,1,2,0:T(8,128)} %copy.74, f32[1,8,8,2,1,256]{5,4,3,1,2,0:T(1,128)S(1)} %copy.73, f32[1,8,8,2,32,255]{5,4,3,1,2,0:T(8,128)} %copy.78, ...), kind=kLoop, calls=%fused_computation.16 | loop fusion | flops 13631488 | bytes 30408720 | tf_op jit(solution)/shard_map/add | solution.py:116
  98.2 27.4 %collective-permute-done.3 = f32[1,8,2,32,256]{4,3,2,1,0:T(8,128)} collective-permute-done((f32[1,8,2,32,256]{4,3,2,1,0:T(8,128)S(1)}, f32[1,8,2,32,256]{4,3,2,1,0:T(8,128)}, u32[]{:S(2)}, u32[]{:S(2)}) %collective-permute-start.3) | collective-permute-done | bytes 524320 | tf_op jit(solution)/shard_map/ppermute | solution.py:123
  127.4 7.3 collective-permute-done.4
  142.2 5.0 gather_fusion
  159.2 5.4 copy.81
  170.4 93.2 %all-to-all-done = f32[1,8,2,256,256]{4,2,1,0,3:T(2,128)} async-done(((f32[1,8,2,256,256]{4,2,1,0,3:T(2,128)}), f32[1,8,2,256,256]{4,2,1,0,3:T(2,128)}, u32[]{:S(2)}, u32[]{:S(2)}) %all-to-all-start) | async-done | bytes 4194336 | tf_op jit(solution)/shard_map/all_to_all | solution.py:132
  263.6 6.0 fusion.6
  279.4 5.3 copy.84
  284.7 185.7 %all_to_all.51 = f32[2,32,2,64,256]{4,3,2,0,1:T(8,128)S(1)} all-to-all(f32[2,32,2,64,256]{4,3,2,0,1:T(8,128)S(1)} %copy.84), channel_id=1, replica_groups=mesh['grp'=2,'px'=4,'py'=4] {'py'}, dimensions={1} | all-to-all | bytes 16777216 | tf_op jit(solution)/shard_map/all_to_all | solution.py:143
  471.5 9.7 %fusion.45 = f32[256,2,8,2,256]{4,0,3,2,1:T(8,128)S(1)} fusion(f32[2,8,2,256,256]{4,3,2,1,0:T(8,128)S(1)} %bitcast.134), kind=kOutput, calls=%fused_computation.84 | convolution fusion | flops 6443499520 | bytes 16777216 | tf_op jit(solution)/shard_map/ctbxy,kx->ctbky/dot_general | solution.py:61
  481.2 8.1 %fusion = f32[2,8,2,256,256]{4,3,2,1,0:T(8,128)S(1)} fusion(f32[256,2,8,2,256]{4,0,3,2,1:T(8,128)S(1)} %fusion.45), kind=kOutput, calls=%fused_computation.6 | convolution fusion | flops 6443499520 | bytes 16777216 | tf_op jit(solution)/shard_map/ctbxy,ky->ctbxk/dot_general | solution.py:62
  499.8 10.0 %fusion.106 = (f32[1,8,2,256,256]{4,3,2,1,0:T(8,128)S(1)}, f32[1,8,2,256,256]{4,3,2,1,0:T(8,128)}, f32[1,8,2,256,256]{4,3,2,1,0:T(8,128)}) fusion(f32[2,8,2,256,256]{4,3,2,1,0:T(8,128)} %copy-done, f32[1,8,2,1,256]{4,3,2,1,0:T(1,128)S(1)} %slice_bitcast_fusion.3, f32[1,8,2,255,256]{4,3,2,1,0:T(8,128)} %slice_bitcast_fusion.1, ...), kind=kLoop, calls=%fused_computation.159 | loop fusion | flops 4194304 | bytes 29360128 | tf_op jit(solution)/shard_map/slice | solution.py:150
  509.8 9.7 %pad_maximum_fusion = f32[3,8,2,256,256]{4,3,2,1,0:T(8,128)} fusion(f32[1,8,2,256,256]{4,3,2,1,0:T(8,128)} %get-tuple-element.16, f32[1,8,2,256,256]{4,3,2,1,0:T(8,128)} %get-tuple-element.15, f32[1,8,2,256,256]{4,3,2,1,0:T(8,128)S(1)} %get-tuple-element.14), kind=kLoop, calls=%fused_computation.1 | loop fusion | flops 6291456 | bytes 25165824 | tf_op jit(solution)/shard_map/stack | solution.py:148
  519.5 21.0 %copy.89 = f32[3,8,2,256,256]{4,2,1,0,3:T(2,128)S(1)} copy(f32[3,8,2,256,256]{4,3,2,1,0:T(8,128)} %pad_maximum_fusion) | data formatting | bytes 25165824 | tf_op jit(solution)/shard_map/stack | solution.py:148
  540.5 143.9 %all_to_all.52 = f32[3,8,2,256,256]{4,2,1,0,3:T(2,128)} all-to-all(f32[3,8,2,256,256]{4,2,1,0,3:T(2,128)S(1)} %copy.89), channel_id=1, replica_groups=mesh['grp'=2,'px'=4,'py'=4] {'grp','px'}, dimensions={3} | all-to-all | bytes 25165824 | tf_op jit(solution)/shard_map/all_to_all | solution.py:155
  684.4 16.6 %copy.90 = f32[3,8,8,2,32,256]{5,4,3,2,1,0:T(8,128)} copy(f32[3,8,8,2,32,256]{5,3,1,0,4,2:T(2,128)} %bitcast.132) | data formatting | bytes 25165824 | tf_op jit(solution)/shard_map/all_to_all | solution.py:155
  701.0 14.9 %add.250 = f32[3,8,16,32,256]{4,3,2,1,0:T(8,128)} add(f32[3,8,16,32,256]{4,3,2,1,0:T(8,128)} %bitcast.128, f32[3,8,16,32,256]{4,3,2,1,0:T(8,128)} %param.4) | non-fusion elementwise | flops 3145728 | bytes 37748736 | tf_op jit(solution)/shard_map/add | solution.py:156
  715.9 14.8 %subtract_select_fusion = (f32[1,8,16,32,256]{4,3,2,1,0:T(8,128)}, f32[1,8,16,32,256]{4,3,2,1,0:T(8,128)S(1)}, pred[1,8,16,32,256]{4,3,2,1,0:T(8,128)(4,1)S(1)}) fusion(f32[3,8,16,32,256]{4,3,2,1,0:T(8,128)} %add.250), kind=kLoop, calls=%fused_computation.10 | loop fusion | flops 55574528 | bytes 22020096 | tf_op jit(solution)/shard_map/jit(_where)/select_n | solution.py:91
  730.7 7.6 %divide_select_fusion.1 = (f32[1,8,16,32,256]{4,3,2,1,0:T(8,128)}, f32[1,8,16,32,256]{4,3,2,1,0:T(8,128)}) fusion(pred[1,8,16,32,256]{4,3,2,1,0:T(8,128)(4,1)S(1)} %get-tuple-element.6, f32[1,8,16,32,256]{4,3,2,1,0:T(8,128)S(1)} %get-tuple-element.5, f32[3,8,16,32,256]{4,3,2,1,0:T(8,128)} %add.250), kind=kLoop, calls=%fused_computation.9 | loop fusion | flops 4194304 | bytes 22020096 | tf_op jit(solution)/shard_map/jit(_where)/select_n | solution.py:92
  739.5 14.4 %subtract_add_fusion = (f32[3,8,16,32,256]{4,3,2,1,0:T(8,128)}, f32[3,8,16,32,256]{4,3,2,1,0:T(8,128)}) fusion(f32[3,8,16,32,256]{4,3,2,1,0:T(8,128)S(1)} %bitcast.127, f32[3,8,16,32,256]{4,3,2,1,0:T(8,128)S(1)} %bitcast.131, f32[1,8,16,32,256]{4,3,2,1,0:T(8,128)} %get-tuple-element.8, f32[1,8,16,32,256]{4,3,2,1,0:T(8,128)} %get-tuple-element.7, ...), kind=kLoop, calls=%fused_computation.4 | loop fusion | flops 12582912 | bytes 62914560 | tf_op jit(solution)/shard_map/add | solution.py:158
  (95 shorter events, 86.4 us)
Async XLA Ops:
  24.1 2.0 copy-start.2
  27.5 35.6 %collective-permute-start = (f32[1,16,32,256]{3,0,1,2:T(1,128)}, f32[1,16,32,256]{3,0,1,2:T(1,128)}, u32[]{:S(2)}, u32[]{:S(2)}) collective-permute-start(f32[1,16,32,256]{3,0,1,2:T(1,128)} %slice.85), channel_id=1, source_target_pairs={{0,1},{1,2},{2,3},{4,5},{5,6},{6,7},{8,9},{9,10},{10,11},{12,13},{... | collective-permute-start | bytes 1572872 | tf_op jit(solution)/shard_map/ppermute | solution.py:27
  39.7 1.9 copy-start.5
  41.6 3.2 copy-start.7
  41.6 21.4 %collective-permute-start.1 = (f32[8,16,1,256]{3,0,1,2:T(8,128)S(1)}, f32[8,16,1,256]{3,0,1,2:T(8,128)S(1)}, u32[]{:S(2)}, u32[]{:S(2)}) collective-permute-start(f32[8,16,1,256]{3,0,1,2:T(8,128)S(1)} %slice.88), channel_id=1, source_target_pairs={{28,0},{0,4},{4,8},{8,12},{12,16},{16,20},{20,24},{24,28},{29,1},{... | collective-permute-start | bytes 393224 | tf_op jit(solution)/shard_map/ppermute | solution.py:33
  42.2 3.5 copy-start.3
  49.5 4.3 copy-start.1
  56.4 8.1 %copy-start.6 = (f32[16,32,256]{2,1,0:T(8,128)S(1)}, f32[16,32,256]{2,1,0:T(8,128)}, u32[]{:S(2)}) copy-start(f32[16,32,256]{2,1,0:T(8,128)} %param.7) | copy-start | bytes 1572868
  83.4 2.0 copy-start.4
  86.6 8.2 %collective-permute-start.2 = (f32[1,8,2,32,256]{4,3,2,1,0:T(8,128)}, f32[1,8,2,32,256]{4,3,2,1,0:T(8,128)}, u32[]{:S(2)}, u32[]{:S(2)}) collective-permute-start(f32[1,8,2,32,256]{4,3,2,1,0:T(8,128)} %get-tuple-element.23), channel_id=1, source_target_pairs={{0,4},{4,0},{8,12},{12,8},{16,20},{20,16},{24,28},{28,24},{1,5},{5... | collective-permute-start | bytes 1572872 | tf_op jit(solution)/shard_map/ppermute | solution.py:123
  88.1 37.4 %collective-permute-start.3 = (f32[1,8,2,32,256]{4,3,2,1,0:T(8,128)S(1)}, f32[1,8,2,32,256]{4,3,2,1,0:T(8,128)}, u32[]{:S(2)}, u32[]{:S(2)}) collective-permute-start(f32[1,8,2,32,256]{4,3,2,1,0:T(8,128)S(1)} %get-tuple-element.22), channel_id=1, source_target_pairs={{0,8},{4,12},{8,0},{12,4},{16,24},{20,28},{24,16},{28,20},{1,9},{5... | collective-permute-start | bytes 1572872 | tf_op jit(solution)/shard_map/ppermute | solution.py:123
  89.6 45.1 %collective-permute-start.4 = (f32[1,8,2,32,256]{4,3,2,1,0:T(8,128)S(1)}, f32[1,8,2,32,256]{4,3,2,1,0:T(8,128)S(1)}, u32[]{:S(2)}, u32[]{:S(2)}) collective-permute-start(f32[1,8,2,32,256]{4,3,2,1,0:T(8,128)S(1)} %get-tuple-element.21), channel_id=1, source_target_pairs={{0,12},{4,8},{8,4},{12,0},{16,28},{20,24},{24,20},{28,16},{1,13},{... | collective-permute-start | bytes 1572872 | tf_op jit(solution)/shard_map/ppermute | solution.py:123
  91.6 49.9 %collective-permute-start.8 = (f32[1,8,2,32,256]{4,3,2,1,0:T(8,128)S(1)}, f32[1,8,2,32,256]{4,3,2,1,0:T(8,128)S(1)}, u32[]{:S(2)}, u32[]{:S(2)}) collective-permute-start(f32[1,8,2,32,256]{4,3,2,1,0:T(8,128)S(1)} %get-tuple-element.17), channel_id=1, source_target_pairs={{0,28},{4,24},{8,20},{12,16},{16,12},{20,8},{24,4},{28,0},{1,29},{... | collective-permute-start | bytes 1572872 | tf_op jit(solution)/shard_map/ppermute | solution.py:123
  93.3 47.3 %collective-permute-start.7 = (f32[1,8,2,32,256]{4,3,2,1,0:T(8,128)S(1)}, f32[1,8,2,32,256]{4,3,2,1,0:T(8,128)S(1)}, u32[]{:S(2)}, u32[]{:S(2)}) collective-permute-start(f32[1,8,2,32,256]{4,3,2,1,0:T(8,128)S(1)} %get-tuple-element.18), channel_id=1, source_target_pairs={{0,24},{4,28},{8,16},{12,20},{16,8},{20,12},{24,0},{28,4},{1,25},{... | collective-permute-start | bytes 1572872 | tf_op jit(solution)/shard_map/ppermute | solution.py:123
  94.8 40.8 %collective-permute-start.5 = (f32[1,8,2,32,256]{4,3,2,1,0:T(8,128)S(1)}, f32[1,8,2,32,256]{4,3,2,1,0:T(8,128)S(1)}, u32[]{:S(2)}, u32[]{:S(2)}) collective-permute-start(f32[1,8,2,32,256]{4,3,2,1,0:T(8,128)S(1)} %get-tuple-element.20), channel_id=1, source_target_pairs={{0,16},{4,20},{8,24},{12,28},{16,0},{20,4},{24,8},{28,12},{1,17},{... | collective-permute-start | bytes 1572872 | tf_op jit(solution)/shard_map/ppermute | solution.py:123
  125.5 14.2 %collective-permute-start.6 = (f32[1,8,2,32,256]{4,3,2,1,0:T(8,128)S(1)}, f32[1,8,2,32,256]{4,3,2,1,0:T(8,128)S(1)}, u32[]{:S(2)}, u32[]{:S(2)}) collective-permute-start(f32[1,8,2,32,256]{4,3,2,1,0:T(8,128)S(1)} %get-tuple-element.19), channel_id=1, source_target_pairs={{0,20},{4,16},{8,28},{12,24},{16,4},{20,0},{24,12},{28,8},{1,21},{... | collective-permute-start | bytes 1572872 | tf_op jit(solution)/shard_map/ppermute | solution.py:123
  164.7 98.9 %all-to-all-start = ((f32[1,8,2,256,256]{4,2,1,0,3:T(2,128)}), f32[1,8,2,256,256]{4,2,1,0,3:T(2,128)}, u32[]{:S(2)}, u32[]{:S(2)}) async-start(f32[1,8,2,256,256]{4,2,1,0,3:T(2,128)} %copy.81), calls=%async_computation | async-start | bytes 8388608 | tf_op jit(solution)/shard_map/all_to_all | solution.py:132
  489.4 3.4 copy-start
  715.9 22.4 %slice-start = ((s8[12582912]{0:T(1024)(128)(4,1)}), s8[4194304]{0:T(1024)(128)(4,1)S(1)}, s32[]{:S(2)}) async-start(s8[12582912]{0:T(1024)(128)(4,1)} %bitcast.126), calls=%async_computation.3 | async-start | bytes 8388608
  715.9 22.4 %slice-start.1 = ((s8[12582912]{0:T(1024)(128)(4,1)}), s8[4194304]{0:T(1024)(128)(4,1)S(1)}, s32[]{:S(2)}) async-start(s8[12582912]{0:T(1024)(128)(4,1)} %bitcast.126), calls=%async_computation.4 | async-start | bytes 8388608
  715.9 22.4 %slice-start.3 = ((s8[12582912]{0:T(1024)(128)(4,1)}), s8[4194304]{0:T(1024)(128)(4,1)S(1)}, s32[]{:S(2)}) async-start(s8[12582912]{0:T(1024)(128)(4,1)} %bitcast.129), calls=%async_computation.6 | async-start | bytes 8388608
  715.9 22.4 %slice-start.4 = ((s8[12582912]{0:T(1024)(128)(4,1)}), s8[4194304]{0:T(1024)(128)(4,1)S(1)}, s32[]{:S(2)}) async-start(s8[12582912]{0:T(1024)(128)(4,1)} %bitcast.129), calls=%async_computation.7 | async-start | bytes 8388608
  730.7 7.6 %slice-start.2 = ((s8[12582912]{0:T(1024)(128)(4,1)}), s8[4194304]{0:T(1024)(128)(4,1)S(1)}, s32[]{:S(2)}) async-start(s8[12582912]{0:T(1024)(128)(4,1)} %bitcast.126), calls=%async_computation.5 | async-start | bytes 8388608
  730.7 8.8 %slice-start.5 = ((s8[12582912]{0:T(1024)(128)(4,1)}), s8[4194304]{0:T(1024)(128)(4,1)S(1)}, s32[]{:S(2)}) async-start(s8[12582912]{0:T(1024)(128)(4,1)} %bitcast.129), calls=%async_computation.8 | async-start | bytes 8388608
